TPU v7x, 32 devices: a whole 2x2x4 slice. The times are simulated.
32 devices in a mesh: expert: 8 (over z, x), hidden: 4 (over y, core).
Axes of the slice: x: 2, y: 2, z: 4, core: 2. Of those that a mesh axis runs over, the one named last changes fastest.
Arguments:
- tokens: bfloat16 [2, 16384, 512], P(None, ('expert', 'hidden')), may hold values from -6 to 6
- grad_out: bfloat16 [2, 16384, 512], P(None, ('expert', 'hidden')), may hold values from -6 to 6
- attn_routes: int32 [2, 16384, 4], P(None, ('expert', 'hidden')), may hold values from 0 to 23, all different within a row
- ffn_routes: int32 [2, 16384, 2], P(None, ('expert', 'hidden')), may hold values from 0 to 15, all different within a row; in each aligned block of 512 rows (0 to 511, 512 to 1023, ..., all dimensions but the last counted through in order) at most 128 rows name the same one
- segments: int32 [2, 64, 256], P(None, ('expert', 'hidden')), may hold values from 0 to 3, never falling along the last dimension, each value on 1 to 128 neighbouring positions
- pad_mask: int32 [2, 16384], P(None, ('expert', 'hidden')), may hold values 0 or 1
- norm1_gain: float32 [512], replicated, may hold values from 0.5 to 1.5
- norm1_bias: float32 [512], replicated, may hold values from -0.6 to 0.6
- attn_router: bfloat16 [512, 24], replicated, may hold values from -0.125 to 0.125
- query_w: bfloat16 [512, 1536], replicated, may hold values from -0.25 to 0.25
- key_w: bfloat16 [512, 64], replicated, may hold values from -0.25 to 0.25
- value_w: bfloat16 [512, 64], replicated, may hold values from -0.25 to 0.25
- attn_proj: bfloat16 [1536, 512], replicated, may hold values from -2 to 2
- norm2_gain: float32 [512], replicated, may hold values from 0.5 to 1.5
- norm2_bias: float32 [512], replicated, may hold values from -0.6 to 0.6
- ffn_router: bfloat16 [512, 16], replicated, may hold values from -0.1875 to 0.1875
- expert_in: bfloat16 [16, 512, 2048], P('expert', None, 'hidden'), may hold values from -0.25 to 0.25
- expert_out: bfloat16 [16, 2048, 512], P('expert', 'hidden'), may hold values from -0.1875 to 0.1875
- halt_w: float32 [512], replicated, may hold values from -0.25 to 0.25
- halt_b: float32 [1], replicated, may hold values from -2.5 to 2.5
Outputs:
- result: bfloat16 [2, 16384, 512], P(None, ('expert', 'hidden'))
- grad_tokens: float32 [2, 16384, 512], P(None, ('expert', 'hidden'))
- grad_norm1_gain: float32 [512], replicated
- grad_norm1_bias: float32 [512], replicated
- grad_attn_router: float32 [512, 24], replicated
- grad_query_w: float32 [512, 1536], replicated
- grad_key_w: float32 [512, 64], replicated
- grad_value_w: float32 [512, 64], replicated
- grad_attn_proj: float32 [1536, 512], replicated
- grad_norm2_gain: float32 [512], replicated
- grad_norm2_bias: float32 [512], replicated
- grad_ffn_router: float32 [512, 16], replicated
- grad_expert_in: float32 [16, 512, 2048], P('expert', None, 'hidden')
- grad_expert_out: float32 [16, 2048, 512], P('expert', 'hidden')
- grad_halt_w: float32 [512], replicated
- grad_halt_b: float32 [1], replicated
Inputs may be any that keep to these rules, and one draw needn't show every extreme that they name: `attn_routes`: each token names 4 different attention experts. `ffn_routes`: each token names 2 different feed-forward experts; in each micro-batch the 512 tokens of one device name no expert more than 128 times, a bound that some block reaches. `segments`: along a packed row the numbers never fall, and each of the 4 numbers covers 1 to 128 positions.
All inputs are finite; a program needn't handle non-finite values. No bound on the sum of `pad_mask` on one device may be relied on, other than what follows from the above.
Results may differ from a plain program's by a relative error of at most 0.015.
The roundings to bfloat16 on the way count: a program that leaves them out, or rounds other values in their place, can miss the bound.
Values may be sent and summed in bfloat16 or wider, within the bound.
A program may use at most 256 MiB of HBM per device.

v0:
```python
import jax
import jax.numpy as jnp
from jax import lax
from jax.sharding import PartitionSpec as P

SEQ = 256
ATT_BLOCK = 512


def layer_norm(value, gain, shift):
    center = value - jnp.mean(value, axis=-1, keepdims=True)
    spread = jnp.mean(center * center, axis=-1, keepdims=True)
    return center * lax.rsqrt(spread + 1e-05) * gain + shift


def norm_back(value, gain, shift, grad):
    unused, pullback = jax.vjp(layer_norm, value, gain, shift)
    return pullback(grad)


def gelu_back(pre, grad):
    unused, pullback = jax.vjp(jax.nn.gelu, pre)
    return pullback(grad)[0]


def softmax_back(probs, grad):
    return probs * (grad - jnp.sum(probs * grad, axis=-1, keepdims=True))


def spread_picks(pick, values):
    total = pick[:, 0, :, None] * values[:, 0, None, :]
    for which in range(1, pick.shape[1]):
        total = total + pick[:, which, :, None] * values[:, which, None, :]
    return total


def masked_scores(query_sel, keys, segment, padding):
    place = jnp.arange(segment.shape[0])
    same_row = place[:, None] // SEQ == place[None, :] // SEQ
    same_pair = segment[:, None] == segment[None, :]
    visible = (padding[None, :] == 1) | (place[:, None] == place[None, :])
    allowed = same_row & same_pair & visible
    scale = keys.shape[1] ** (-0.5)
    scores = jnp.einsum("qkh,jh->qkj", query_sel, keys, preferred_element_type=jnp.float32) * scale
    return jnp.where(allowed[:, None, :], scores, -1e30)


def attend_forward(operands):
    query_sel, keys, values, segment, padding = operands
    scores = masked_scores(query_sel, keys, segment, padding)
    top = jnp.max(scores, axis=-1, keepdims=True)
    expo = jnp.exp(scores - top)
    total = jnp.sum(expo, axis=-1, keepdims=True)
    probs = (expo / total).astype(jnp.bfloat16)
    heads = jnp.einsum("qkj,jh->qkh", probs, values, preferred_element_type=jnp.float32)
    return (heads, top + jnp.log(total))


def attend_backward(operands):
    query_sel, keys, values, segment, padding, logsum, grad_heads = operands
    scale = keys.shape[1] ** (-0.5)
    probs = jnp.exp(masked_scores(query_sel, keys, segment, padding) - logsum)
    probs_low = probs.astype(jnp.bfloat16)
    grad_values = jnp.einsum(
        "qkj,qkh->jh", probs_low, grad_heads, preferred_element_type=jnp.float32
    )
    grad_probs = jnp.einsum("qkh,jh->qkj", grad_heads, values, preferred_element_type=jnp.float32)
    grad_scores = softmax_back(probs, grad_probs).astype(jnp.bfloat16)
    grad_query = (
        jnp.einsum("qkj,jh->qkh", grad_scores, keys, preferred_element_type=jnp.float32) * scale
    )
    grad_keys = (
        jnp.einsum("qkj,qkh->jh", grad_scores, query_sel, preferred_element_type=jnp.float32)
        * scale
    )
    return (grad_query, grad_keys, grad_values)


def expert_forward(rows, first, second):
    pre = jnp.einsum("erd,edf->erf", rows, first, preferred_element_type=jnp.float32)
    act = jax.nn.gelu(pre).astype(jnp.bfloat16)
    total = jnp.einsum("erf,efd->erd", act, second, preferred_element_type=jnp.float32)
    return (pre, act, total)


def expert_backward(rows, pre, act, grad_rows_in, first, second):
    grad_act = jnp.einsum("erd,efd->erf", grad_rows_in, second, preferred_element_type=jnp.float32)
    grad_pre = gelu_back(pre, grad_act).astype(jnp.bfloat16)
    grad_second = jnp.einsum("erf,erd->efd", act, grad_rows_in, preferred_element_type=jnp.float32)
    grad_first = jnp.einsum("erd,erf->edf", rows, grad_pre, preferred_element_type=jnp.float32)
    grad_rows_out = jnp.einsum("erf,edf->erd", grad_pre, first, preferred_element_type=jnp.float32)
    return (grad_first, grad_second, grad_rows_out)


def per_device(
    tokens,
    grad_out,
    attn_routes,
    ffn_routes,
    segments,
    pad_mask,
    norm1_gain,
    norm1_bias,
    attn_router,
    query_w,
    key_w,
    value_w,
    attn_proj,
    norm2_gain,
    norm2_bias,
    ffn_router,
    expert_in,
    expert_out,
    halt_w,
    halt_b,
):
    micro_count, tok_rows, width = tokens.shape
    att_count = attn_router.shape[1]
    head = key_w.shape[1]
    experts_all = ffn_router.shape[1]
    top_ffn = ffn_routes.shape[2]
    capacity = 4 * tok_rows // experts_all
    blocks = tok_rows // ATT_BLOCK
    f32 = jnp.float32
    bf16 = jnp.bfloat16
    full_in, full_out = (
        lax.all_gather(expert_in, "hidden", axis=2, tiled=True),
        lax.all_gather(expert_out, "hidden", axis=1, tiled=True),
    )
    acc_in = jnp.zeros(full_in.shape, f32)
    acc_out = jnp.zeros(full_out.shape, f32)
    totals = (
        jnp.zeros(norm1_gain.shape, f32),
        jnp.zeros(norm1_bias.shape, f32),
        jnp.zeros(attn_router.shape, f32),
        jnp.zeros(query_w.shape, f32),
        jnp.zeros(key_w.shape, f32),
        jnp.zeros(value_w.shape, f32),
        jnp.zeros(attn_proj.shape, f32),
        jnp.zeros(norm2_gain.shape, f32),
        jnp.zeros(norm2_bias.shape, f32),
        jnp.zeros(ffn_router.shape, f32),
        jnp.zeros(halt_w.shape, f32),
        jnp.zeros(halt_b.shape, f32),
    )
    results = []
    grads_in = []
    for micro in range(micro_count):
        state_in = tokens[micro].astype(f32)
        segment = segments[micro].reshape(-1)
        padding = pad_mask[micro]
        route_attn = attn_routes[micro]
        route_ffn = ffn_routes[micro]
        normed = layer_norm(state_in, norm1_gain, norm1_bias)
        normed_low = normed.astype(bf16)
        logits_attn = jnp.dot(normed_low, attn_router, preferred_element_type=f32)
        pick_attn = (route_attn[:, :, None] == jnp.arange(att_count)[None, None, :]).astype(f32)
        gate_attn = jax.nn.softmax(jnp.sum(pick_attn * logits_attn[:, None, :], axis=-1), axis=-1)
        query_all = (
            jnp.dot(normed_low, query_w, preferred_element_type=f32)
            .astype(bf16)
            .reshape(tok_rows, att_count, head)
        )
        keys_low = jnp.dot(normed_low, key_w, preferred_element_type=f32).astype(bf16)
        values_low = jnp.dot(normed_low, value_w, preferred_element_type=f32).astype(bf16)
        pick_low = pick_attn.astype(bf16)
        query_sel = jnp.einsum(
            "tke,teh->tkh", pick_low, query_all, preferred_element_type=f32
        ).astype(bf16)
        block_query = query_sel.reshape(blocks, ATT_BLOCK, -1, head)
        block_keys = keys_low.reshape(blocks, ATT_BLOCK, head)
        block_values = values_low.reshape(blocks, ATT_BLOCK, head)
        block_segment = segment.reshape(blocks, ATT_BLOCK)
        block_padding = padding.reshape(blocks, ATT_BLOCK)
        heads, logsum = lax.map(
            attend_forward, (block_query, block_keys, block_values, block_segment, block_padding)
        )
        heads = heads.reshape(tok_rows, -1, head)
        mixed = spread_picks(pick_attn, gate_attn[:, :, None] * heads)
        mixed_low = mixed.reshape(tok_rows, -1).astype(bf16)
        state_mid = state_in + jnp.dot(mixed_low, attn_proj, preferred_element_type=f32)
        normed_two = layer_norm(state_mid, norm2_gain, norm2_bias)
        ffn_low = normed_two.astype(bf16)
        logits_ffn = jnp.dot(ffn_low, ffn_router, preferred_element_type=f32)
        pick_ffn = (route_ffn[:, :, None] == jnp.arange(experts_all)[None, None, :]).astype(f32)
        gate_ffn = jax.nn.softmax(jnp.sum(pick_ffn * logits_ffn[:, None, :], axis=-1), axis=-1)
        flat_route = route_ffn.reshape(-1)
        onehot = (flat_route[:, None] == jnp.arange(experts_all)[None, :]).astype(jnp.int32)
        rank = jnp.sum((jnp.cumsum(onehot, axis=0) - 1) * onehot, axis=1)
        slot = flat_route * capacity + rank
        outgoing = (
            jnp.zeros((experts_all * capacity, width), bf16)
            .at[slot]
            .set(jnp.repeat(ffn_low, top_ffn, axis=0))
        )
        arrived = lax.all_to_all(
            outgoing.reshape(experts_all, capacity, width),
            "expert",
            split_axis=0,
            concat_axis=1,
            tiled=True,
        )
        pre, act, expert_res = expert_forward(arrived, full_in, full_out)
        outgoing_back = expert_res.astype(bf16)
        returned = lax.all_to_all(
            outgoing_back, "expert", split_axis=1, concat_axis=0, tiled=True
        ).reshape(experts_all * capacity, width)
        picked = returned[slot].reshape(tok_rows, top_ffn, width).astype(f32)
        state_end = state_mid + jnp.sum(gate_ffn[:, :, None] * picked, axis=1)
        halting = jax.nn.sigmoid(jnp.sum(state_end * halt_w, axis=-1, keepdims=True) + halt_b)
        branch = state_end - state_in
        results.append((state_in + halting * branch).astype(bf16))
        grad_res = grad_out[micro].astype(f32)
        grad_halt = jnp.sum(grad_res * branch, axis=-1, keepdims=True) * halting * (1.0 - halting)
        grad_end = halting * grad_res + grad_halt * halt_w
        grad_state = grad_res * (1.0 - halting)
        grad_gate_ffn = jnp.sum(picked * grad_end[:, None, :], axis=-1)
        send_grad = (gate_ffn[:, :, None] * grad_end[:, None, :]).astype(bf16).reshape(-1, width)
        grad_buffer = jnp.zeros((experts_all * capacity, width), bf16).at[slot].set(send_grad)
        grad_arrived = lax.all_to_all(
            grad_buffer.reshape(experts_all, capacity, width),
            "expert",
            split_axis=0,
            concat_axis=1,
            tiled=True,
        )
        grad_first, grad_second, grad_rows_out = expert_backward(
            arrived, pre, act, grad_arrived, full_in, full_out
        )
        back_rows = grad_rows_out.astype(bf16)
        acc_in = acc_in + grad_first
        acc_out = acc_out + grad_second
        grad_back = lax.all_to_all(
            back_rows, "expert", split_axis=1, concat_axis=0, tiled=True
        ).reshape(experts_all * capacity, width)
        grad_slots = grad_back[slot].reshape(tok_rows, top_ffn, width).astype(f32)
        grad_sel_ffn = softmax_back(gate_ffn, grad_gate_ffn)
        grad_logits_ffn = jnp.sum(pick_ffn * grad_sel_ffn[:, :, None], axis=1).astype(bf16)
        grad_router_ffn = jnp.dot(ffn_low.T, grad_logits_ffn, preferred_element_type=f32)
        grad_normed_two = jnp.sum(grad_slots, axis=1) + jnp.dot(
            grad_logits_ffn, ffn_router.T, preferred_element_type=f32
        )
        grad_mid_norm, grad_gain_two, grad_bias_two = norm_back(
            state_mid, norm2_gain, norm2_bias, grad_normed_two
        )
        grad_mid = grad_end + grad_mid_norm
        grad_state = grad_state + grad_mid
        grad_attn = grad_mid.astype(bf16)
        grad_proj = jnp.dot(mixed_low.T, grad_attn, preferred_element_type=f32)
        grad_mixed = (
            jnp.dot(grad_attn, attn_proj.T, preferred_element_type=f32)
            .astype(bf16)
            .reshape(tok_rows, att_count, head)
        )
        grad_sel = jnp.einsum("tke,teh->tkh", pick_low, grad_mixed, preferred_element_type=f32)
        grad_gate_attn = jnp.sum(heads * grad_sel, axis=-1)
        grad_heads = (gate_attn[:, :, None] * grad_sel).astype(bf16)
        grad_query, grad_keys, grad_values = lax.map(
            attend_backward,
            (
                block_query,
                block_keys,
                block_values,
                block_segment,
                block_padding,
                logsum,
                grad_heads.reshape(blocks, ATT_BLOCK, -1, head),
            ),
        )
        grad_query_all = (
            spread_picks(pick_attn, grad_query.reshape(tok_rows, -1, head))
            .reshape(tok_rows, -1)
            .astype(bf16)
        )
        grad_keys_low = grad_keys.reshape(tok_rows, head).astype(bf16)
        grad_values_low = grad_values.reshape(tok_rows, head).astype(bf16)
        grad_query_w = jnp.dot(normed_low.T, grad_query_all, preferred_element_type=f32)
        grad_key_w = jnp.dot(normed_low.T, grad_keys_low, preferred_element_type=f32)
        grad_value_w = jnp.dot(normed_low.T, grad_values_low, preferred_element_type=f32)
        grad_sel_attn = softmax_back(gate_attn, grad_gate_attn)
        grad_logits_attn = jnp.sum(pick_attn * grad_sel_attn[:, :, None], axis=1).astype(bf16)
        grad_router_attn = jnp.dot(normed_low.T, grad_logits_attn, preferred_element_type=f32)
        grad_normed = (
            jnp.dot(grad_query_all, query_w.T, preferred_element_type=f32)
            + jnp.dot(grad_keys_low, key_w.T, preferred_element_type=f32)
            + jnp.dot(grad_values_low, value_w.T, preferred_element_type=f32)
            + jnp.dot(grad_logits_attn, attn_router.T, preferred_element_type=f32)
        )
        grad_in_norm, grad_gain_one, grad_bias_one = norm_back(
            state_in, norm1_gain, norm1_bias, grad_normed
        )
        grads_in.append(grad_state + grad_in_norm)
        grad_halt_w = jnp.sum(grad_halt * state_end, axis=0)
        grad_halt_b = jnp.sum(grad_halt, axis=0)
        summed = lax.psum(
            (
                grad_gain_one,
                grad_bias_one,
                grad_router_attn,
                grad_query_w,
                grad_key_w,
                grad_value_w,
                grad_proj,
                grad_gain_two,
                grad_bias_two,
                grad_router_ffn,
                grad_halt_w,
                grad_halt_b,
            ),
            ("expert", "hidden"),
        )
        totals = tuple(jax.tree.map(jnp.add, totals, tuple(summed)))
    acc_in, acc_out = (
        lax.psum_scatter(
            acc_in.astype(jnp.bfloat16), "hidden", scatter_dimension=2, tiled=True
        ).astype(jnp.float32),
        lax.psum_scatter(
            acc_out.astype(jnp.bfloat16), "hidden", scatter_dimension=1, tiled=True
        ).astype(jnp.float32),
    )
    return (
        jnp.stack(results),
        jnp.stack(grads_in),
        totals[0],
        totals[1],
        totals[2],
        totals[3],
        totals[4],
        totals[5],
        totals[6],
        totals[7],
        totals[8],
        totals[9],
        acc_in,
        acc_out,
        totals[10],
        totals[11],
    )


def solution(mesh):
    in_specs = (
        P(None, ("expert", "hidden"), None),
        P(None, ("expert", "hidden"), None),
        P(None, ("expert", "hidden"), None),
        P(None, ("expert", "hidden"), None),
        P(None, ("expert", "hidden"), None),
        P(None, ("expert", "hidden")),
        P(),
        P(),
        P(),
        P(),
        P(),
        P(),
        P(),
        P(),
        P(),
        P(),
        P("expert", None, "hidden"),
        P("expert", "hidden", None),
        P(),
        P(),
    )
    out_specs = (
        P(None, ("expert", "hidden"), None),
        P(None, ("expert", "hidden"), None),
        P(),
        P(),
        P(),
        P(),
        P(),
        P(),
        P(),
        P(),
        P(),
        P(),
        P("expert", None, "hidden"),
        P("expert", "hidden", None),
        P(),
        P(),
    )
    return jax.shard_map(
        per_device, mesh=mesh, in_specs=in_specs, out_specs=out_specs, check_vma=False
    )
```

profile of v0, /device:TPU:0, one launch (start us, length us, event | category | flops | bytes accessed | tf_op | source)
XLA Modules:
  0.0 937.1 jit_solution(10444804443158342972)
XLA Ops:
  27.1 8.9 select_reduce_fusion.3
  38.8 8.9 select_reduce_fusion.2
  58.2 4.5 reduce-window.16
  65.3 4.6 fusion.181
  90.4 4.9 copy.590
  103.1 5.0 copy.613
  134.6 7.2 scatter_custom_fusion.1
  141.8 7.4 all-to-all-start.2
  150.0 4.5 reduce-window.14
  160.8 7.2 scatter_custom_fusion
  168.0 29.6 %all-to-all-done.2 = bf16[16,128,512]{2,1,0:T(8,128)(2,1)} async-done(((bf16[16,128,512]{2,1,0:T(8,128)(2,1)}), bf16[16,128,512]{2,1,0:T(8,128)(2,1)}, u32[]{:S(2)}, u32[]{:S(2)}) %all-to-all-start.2) | async-done | bytes 2097184 | tf_op jit(solution)/shard_map/all_to_all | solution.py:196
  197.6 4.8 all-to-all-start
  205.4 13.1 %fusion.188 = f32[2,1024,2048]{2,1,0:T(8,128)} fusion(bf16[2,1024,512]{2,1,0:T(8,128)(2,1)} %bitcast.422, bf16[2,512,2048]{2,1,0:T(8,128)(2,1)} %all-gather.3.cloned.1.call-done), kind=kOutput, calls=%fused_computation.370 | convolution fusion | flops 4294967296 | bytes 23068672 | tf_op jit(solution)/shard_map/erd,edf->erf/dot_general | solution.py:80
  218.5 10.1 %convolution_convert_fusion.6 = bf16[2,1024,512]{2,1,0:T(8,128)(2,1)S(1)} fusion(bf16[2,2048,512]{2,1,0:T(8,128)(2,1)} %all-gather.5.cloned.1.call-done, f32[2,1024,2048]{2,1,0:T(8,128)} %fusion.188), kind=kOutput, calls=%fused_computation.71 | convolution fusion | flops 4333764608 | bytes 23068672 | tf_op jit(solution)/shard_map/erf,efd->erd/dot_general | solution.py:82
  232.1 18.0 %all-to-all-done = bf16[16,128,512]{2,1,0:T(8,128)(2,1)} async-done(((bf16[16,128,512]{2,1,0:T(8,128)(2,1)}), bf16[16,128,512]{2,1,0:T(8,128)(2,1)}, u32[]{:S(2)}, u32[]{:S(2)}) %all-to-all-start) | async-done | bytes 2097184 | tf_op jit(solution)/shard_map/all_to_all | solution.py:196
  250.1 4.6 all-to-all-start.3
  257.5 10.4 %multiply_convert_fusion.1 = (bf16[2,1024,2048]{2,1,0:T(8,128)(2,1)S(1)}, f32[2,1024,2048]{2,1,0:T(8,128)}) fusion(bf16[2,1024,512]{2,1,0:T(8,128)(2,1)S(1)} %bitcast.424, bf16[2,512,2048]{2,1,0:T(8,128)(2,1)S(1)} %copy-done.202), kind=kOutput, calls=%fused_computation.27 | convolution fusion | flops 4332716032 | bytes 31457280 | tf_op jit(solution)/shard_map/erd,edf->erf/dot_general | solution.py:80
  267.9 4.7 convolution_convert_fusion.7
  276.1 26.4 %all-to-all-done.3 = bf16[2,1024,512]{2,0,1:T(2,128)(2,1)} async-done(((bf16[2,1024,512]{2,0,1:T(2,128)(2,1)}), bf16[2,1024,512]{2,0,1:T(2,128)(2,1)}, u32[]{:S(2)}, u32[]{:S(2)}) %all-to-all-start.3) | async-done | bytes 2097184 | tf_op jit(solution)/shard_map/all_to_all | solution.py:205
  302.5 4.6 all-to-all-start.1
  321.6 7.0 gather_fusion.1
  331.9 5.4 multiply_reduce_fusion.4
  339.8 15.0 %all-to-all-done.1 = bf16[2,1024,512]{2,0,1:T(2,128)(2,1)} async-done(((bf16[2,1024,512]{2,0,1:T(2,128)(2,1)}), bf16[2,1024,512]{2,0,1:T(2,128)(2,1)}, u32[]{:S(2)}, u32[]{:S(2)}) %all-to-all-start.1) | async-done | bytes 2097184 | tf_op jit(solution)/shard_map/all_to_all | solution.py:205
  358.2 7.0 gather_fusion
  368.5 5.4 multiply_reduce_fusion.5
  389.2 8.2 scatter_custom_fusion.2
  411.0 7.7 scatter_custom_fusion.3
  418.8 30.8 %all-to-all-done.4 = bf16[16,128,512]{2,1,0:T(8,128)(2,1)} async-done(((bf16[16,128,512]{2,1,0:T(8,128)(2,1)}), bf16[16,128,512]{2,1,0:T(8,128)(2,1)}, u32[]{:S(2)}, u32[]{:S(2)}) %all-to-all-start.4) | async-done | bytes 2097184 | tf_op jit(solution)/shard_map/all_to_all | solution.py:220
  466.9 12.2 %fusion.194 = f32[2,2048,512]{2,1,0:T(8,128)} fusion(bf16[2,1024,2048]{2,1,0:T(8,128)(2,1)} %copy-done.208, bf16[2,1024,512]{2,1,0:T(8,128)(2,1)S(1)} %bitcast.426), kind=kOutput, calls=%fused_computation.376 | convolution fusion | flops 4294967296 | bytes 18874368 | tf_op jit(solution)/shard_map/erf,erd->efd/dot_general | solution.py:89
  479.1 22.7 %all-to-all-done.6 = bf16[16,128,512]{2,1,0:T(8,128)(2,1)} async-done(((bf16[16,128,512]{2,1,0:T(8,128)(2,1)}), bf16[16,128,512]{2,1,0:T(8,128)(2,1)}, u32[]{:S(2)}, u32[]{:S(2)}) %all-to-all-start.6) | async-done | bytes 2097184 | tf_op jit(solution)/shard_map/all_to_all | solution.py:220
  504.9 13.1 %add_convert_fusion = bf16[2,2048,512]{2,1,0:T(8,128)(2,1)} fusion(f32[2,2048,512]{2,1,0:T(8,128)} %fusion.194, bf16[2,1024,512]{2,1,0:T(8,128)(2,1)S(1)} %bitcast.428, f32[2,1024,2048]{2,1,0:T(8,128)} %fusion.188), kind=kOutput, calls=%fused_computation.28 | convolution fusion | flops 4336910336 | bytes 31457280 | tf_op jit(solution)/shard_map/erf,erd->efd/dot_general | solution.py:89
  518.0 20.5 %fusion.13 = bf16[2,1024,2048]{2,1,0:T(8,128)(2,1)} fusion(f32[2,1024,2048]{2,1,0:T(8,128)} %fusion.188, bf16[2,1024,512]{2,1,0:T(8,128)(2,1)} %bitcast.429, bf16[2,2048,512]{2,1,0:T(8,128)(2,1)} %all-gather.5.cloned.1.call-done), kind=kOutput, calls=%fused_computation.25 | convolution fusion | flops 4378853376 | bytes 31457280 | tf_op jit(solution)/shard_map/erd,efd->erf/dot_general | solution.py:87
  538.5 8.5 convolution_convert_fusion.4
  550.5 4.8 all-to-all-start.7
  555.3 19.9 %fusion.6 = bf16[2,1024,2048]{2,1,0:T(8,128)(2,1)} fusion(f32[2,1024,2048]{2,1,0:T(8,128)} %get-tuple-element.359, bf16[2,1024,512]{2,1,0:T(8,128)(2,1)} %bitcast.427, bf16[2,2048,512]{2,1,0:T(8,128)(2,1)} %all-gather.5.cloned.1.call-done), kind=kOutput, calls=%fused_computation.18 | convolution fusion | flops 4378853376 | bytes 31457280 | tf_op jit(solution)/shard_map/erd,efd->erf/dot_general | solution.py:87
  575.2 8.5 convolution_convert_fusion.5
  587.2 15.7 %all-to-all-done.7 = bf16[2,1024,512]{2,0,1:T(2,128)(2,1)} async-done(((bf16[2,1024,512]{2,0,1:T(2,128)(2,1)}), bf16[2,1024,512]{2,0,1:T(2,128)(2,1)}, u32[]{:S(2)}, u32[]{:S(2)}) %all-to-all-start.7) | async-done | bytes 2097184 | tf_op jit(solution)/shard_map/all_to_all | solution.py:233
  609.6 7.9 fusion.193
  617.5 9.8 %add_convert_fusion.1 = bf16[2,512,2048]{2,1,0:T(8,128)(2,1)} fusion(f32[2,512,2048]{2,1,0:T(8,128)S(1)} %fusion.193, bf16[2,1024,512]{2,1,0:T(8,128)(2,1)S(1)} %bitcast.423, bf16[2,1024,2048]{2,1,0:T(8,128)(2,1)} %fusion.13), kind=kOutput, calls=%fused_computation.29 | convolution fusion | flops 4299161600 | bytes 23068672 | tf_op jit(solution)/shard_map/erd,erf->edf/dot_general | solution.py:90
  630.7 5.8 gather_fusion.3
  636.6 18.5 %all-to-all-done.5 = bf16[2,1024,512]{2,0,1:T(2,128)(2,1)} async-done(((bf16[2,1024,512]{2,0,1:T(2,128)(2,1)}), bf16[2,1024,512]{2,0,1:T(2,128)(2,1)}, u32[]{:S(2)}, u32[]{:S(2)}) %all-to-all-start.5) | async-done | bytes 2097184 | tf_op jit(solution)/shard_map/all_to_all | solution.py:233
  658.4 7.0 gather_fusion.2
  668.7 5.1 reduce_sum.693
  678.9 5.1 reduce_sum.706
  703.5 4.9 copy.641
  716.2 5.2 copy.663
  785.4 40.2 %all-reduce.6 = (f32[512]{0:T(512)}, f32[512]{0:T(512)}, f32[512,24]{0,1:T(8,128)}, f32[512]{0:T(512)}, f32[512]{0:T(512)}, /*index=5*/f32[512,16]{0,1:T(8,128)}, f32[512]{0:T(512)}, f32[1]{0:T(128)}) all-reduce(f32[512]{0:T(512)S(1)} %add.604, f32[512]{0:T(512)S(1)} %add.605, ...), channel_id=1, replica_groups=mesh['expert'=8,'hidden'=4] {'expert','hidden'}, use_global_device_ids=true, to_apply=%region_65.66 | all-reduce | flops 23041 | bytes 184328 | tf_op jit(solution)/shard_map/psum | solution.py:295
  831.4 92.1 %all-reduce.5.cloned.1.call-done = (f32[512,1536]{1,0:T(8,128)}, f32[512,64]{0,1:T(8,128)}, f32[512,64]{0,1:T(8,128)}, f32[1536,512]{1,0:T(8,128)}) async-done(((f32[512,1536]{1,0:T(8,128)}, f32[512,64]{0,1:T(8,128)}, f32[512,64]{0,1:T(8,128)}, f32[1536,512]{1,0:T(8,128)}), (f32[512,1536]{1,0:T(8,128)}, f32[512,64]{0,1:T(8,128)}, f32[512,64]{0,1:T(8,128)}, ...) | async-done | bytes 6553616 | tf_op jit(solution)/shard_map/psum | solution.py:295
  (690 shorter events, 315.2 us)
Async XLA Ops:
  7.2 111.5 %copy-start = (bf16[1536,512]{1,0:T(8,128)(2,1)S(1)}, bf16[1536,512]{1,0:T(8,128)(2,1)}, u32[]{:S(2)}) copy-start(bf16[1536,512]{1,0:T(8,128)(2,1)} %param.32) | copy-start | bytes 4718596
  7.2 198.2 %all-gather.3.cloned.1.call-start = ((), (), s32[]{:S(2)}) async-start(), calls=%async_computation.10 | async-start | bytes 5242880 | tf_op jit(solution)/shard_map/all_gather | solution.py:127
  7.9 210.6 %all-gather.5.cloned.1.call-start = ((), (), s32[]{:S(2)}) async-start(), calls=%async_computation.11 | async-start | bytes 5242880 | tf_op jit(solution)/shard_map/all_gather | solution.py:128
  13.8 441.7 %copy-start.5 = (bf16[1,512,512]{1,2,0:T(8,128)(2,1)}, bf16[1,512,512]{1,2,0:T(8,128)(2,1)S(1)}, u32[]{:S(2)}) copy-start(bf16[1,512,512]{1,2,0:T(8,128)(2,1)S(1)} %copy.704) | copy-start | bytes 1572868
  14.3 365.7 %copy-start.7 = (bf16[1,512,512]{1,2,0:T(8,128)(2,1)}, bf16[1,512,512]{1,2,0:T(8,128)(2,1)S(1)}, u32[]{:S(2)}) copy-start(bf16[1,512,512]{1,2,0:T(8,128)(2,1)S(1)} %copy.705) | copy-start | bytes 1572868
  15.7 38.6 %copy-start.14 = (bf16[512,512]{0,1:T(8,128)(2,1)}, bf16[512,512]{0,1:T(8,128)(2,1)S(1)}, u32[]{:S(2)}) copy-start(bf16[512,512]{0,1:T(8,128)(2,1)S(1)} %get-tuple-element.333) | copy-start | bytes 1572868
  15.9 104.8 %copy-start.73 = (bf16[512,64,1]{0,1,2:T(8,128)(2,1)}, bf16[512,64,1]{0,1,2:T(8,128)(2,1)S(1)}, u32[]{:S(2)}) copy-start(bf16[512,64,1]{0,1,2:T(8,128)(2,1)S(1)} %fusion.62) | copy-start | bytes 196612
  17.0 97.3 %copy-start.75 = (bf16[512,64,1]{0,1,2:T(8,128)(2,1)}, bf16[512,64,1]{0,1,2:T(8,128)(2,1)S(1)}, u32[]{:S(2)}) copy-start(bf16[512,64,1]{0,1,2:T(8,128)(2,1)S(1)} %fusion.64) | copy-start | bytes 196612
  20.1 75.2 %copy-start.44 = (s32[512,4]{1,0:T(8,128)}, s32[512,4]{1,0:T(8,128)S(1)}, u32[]{:S(2)}) copy-start(s32[512,4]{1,0:T(8,128)S(1)} %copy.585) | copy-start | bytes 24580
  37.1 47.5 %copy-start.105 = (f32[512,4]{0,1:T(4,128)}, f32[512,4]{0,1:T(4,128)S(1)}, u32[]{:S(2)}) copy-start(f32[512,4]{0,1:T(4,128)S(1)} %copy.588) | copy-start | bytes 24580
  50.4 36.7 %copy-start.103 = (f32[512,4]{0,1:T(4,128)}, f32[512,4]{0,1:T(4,128)S(1)}, u32[]{:S(2)}) copy-start(f32[512,4]{0,1:T(4,128)S(1)} %copy.611) | copy-start | bytes 24580
  87.8 27.9 %copy-start.122 = (f32[512,4]{0,1:T(4,128)}, f32[512,4]{0,1:T(4,128)S(1)}, u32[]{:S(2)}) copy-start(f32[512,4]{0,1:T(4,128)S(1)} %fusion.156) | copy-start | bytes 24580
  100.4 20.3 %copy-start.53 = (bf16[512,4,64]{0,2,1:T(8,128)(2,1)}, bf16[512,4,64]{0,2,1:T(8,128)(2,1)S(1)}, u32[]{:S(2)}) copy-start(bf16[512,4,64]{0,2,1:T(8,128)(2,1)S(1)} %copy.591) | copy-start | bytes 786436
  128.4 13.4 %copy-start.38 = (bf16[512,512]{0,1:T(8,128)(2,1)}, bf16[512,512]{0,1:T(8,128)(2,1)S(1)}, u32[]{:S(2)}) copy-start(bf16[512,512]{0,1:T(8,128)(2,1)S(1)} %get-tuple-element.329) | copy-start | bytes 1572868
  134.6 14.6 %copy-start.187 = (s32[1,512,2]{1,2,0:T(2,128)S(1)}, s32[1,512,2]{1,2,0:T(2,128)}, u32[]{:S(2)}) copy-start(s32[1,512,2]{1,2,0:T(2,128)} %get-tuple-element.327) | copy-start | bytes 12292
  134.6 15.1 %copy-start.186 = (s32[1,512,2]{1,2,0:T(2,128)S(1)}, s32[1,512,2]{1,2,0:T(2,128)}, u32[]{:S(2)}) copy-start(s32[1,512,2]{1,2,0:T(2,128)} %get-tuple-element.323) | copy-start | bytes 12292
  141.8 13.1 %copy-start.40 = (bf16[512,512]{0,1:T(8,128)(2,1)S(1)}, bf16[512,512]{0,1:T(8,128)(2,1)}, u32[]{:S(2)}) copy-start(bf16[512,512]{0,1:T(8,128)(2,1)} %get-tuple-element.328) | copy-start | bytes 1572868
  141.8 55.7 %all-to-all-start.2 = ((bf16[16,128,512]{2,1,0:T(8,128)(2,1)}), bf16[16,128,512]{2,1,0:T(8,128)(2,1)}, u32[]{:S(2)}, u32[]{:S(2)}) async-start(bf16[16,128,512]{2,1,0:T(8,128)(2,1)} %bitcast.410), calls=%async_computation.2 | async-start | bytes 4194304 | tf_op jit(solution)/shard_map/all_to_all | solution.py:196
  197.6 52.6 %all-to-all-start = ((bf16[16,128,512]{2,1,0:T(8,128)(2,1)}), bf16[16,128,512]{2,1,0:T(8,128)(2,1)}, u32[]{:S(2)}, u32[]{:S(2)}) async-start(bf16[16,128,512]{2,1,0:T(8,128)(2,1)} %bitcast.411), calls=%async_computation | async-start | bytes 4194304 | tf_op jit(solution)/shard_map/all_to_all | solution.py:196
  250.1 52.3 %all-to-all-start.3 = ((bf16[2,1024,512]{2,0,1:T(2,128)(2,1)}), bf16[2,1024,512]{2,0,1:T(2,128)(2,1)}, u32[]{:S(2)}, u32[]{:S(2)}) async-start(bf16[2,1024,512]{2,0,1:T(2,128)(2,1)} %copy.627), calls=%async_computation.3 | async-start | bytes 4194304 | tf_op jit(solution)/shard_map/all_to_all | solution.py:205
  256.6 11.3 %copy-start.62 = (bf16[2,8,128,512]{3,2,1,0:T(8,128)(2,1)}, bf16[2,8,128,512]{3,2,1,0:T(8,128)(2,1)S(1)}, u32[]{:S(2)}) copy-start(bf16[2,8,128,512]{3,2,1,0:T(8,128)(2,1)S(1)} %copy.603) | copy-start | bytes 6291460
  257.5 10.4 %copy-start.205 = (bf16[2,2048,512]{2,1,0:T(8,128)(2,1)S(1)}, bf16[2,2048,512]{2,1,0:T(8,128)(2,1)}, u32[]{:S(2)}) copy-start(bf16[2,2048,512]{2,1,0:T(8,128)(2,1)} %all-gather.5.cloned.1.call-done) | copy-start | bytes 12582916
  302.5 52.4 %all-to-all-start.1 = ((bf16[2,1024,512]{2,0,1:T(2,128)(2,1)}), bf16[2,1024,512]{2,0,1:T(2,128)(2,1)}, u32[]{:S(2)}, u32[]{:S(2)}) async-start(bf16[2,1024,512]{2,0,1:T(2,128)(2,1)} %copy.604), calls=%async_computation.1 | async-start | bytes 4194304 | tf_op jit(solution)/shard_map/all_to_all | solution.py:205
  311.2 68.9 %copy-start.18 = (bf16[1,512,512]{1,2,0:T(8,128)(2,1)}, bf16[1,512,512]{1,2,0:T(8,128)(2,1)S(1)}, u32[]{:S(2)}) copy-start(bf16[1,512,512]{1,2,0:T(8,128)(2,1)S(1)} %copy.706) | copy-start | bytes 1572868
  318.2 39.9 %copy-start.140 = (s32[1024]{0:T(1024)}, s32[1024]{0:T(1024)S(1)}, u32[]{:S(2)}) copy-start(s32[1024]{0:T(1024)S(1)} %broadcast_clamp_fusion.1) | copy-start | bytes 12292
  318.3 10.3 %copy-start.142 = (s32[1024]{0:T(1024)}, s32[1024]{0:T(1024)S(1)}, u32[]{:S(2)}) copy-start(s32[1024]{0:T(1024)S(1)} %broadcast_clamp_fusion) | copy-start | bytes 12292
  397.3 52.3 %all-to-all-start.4 = ((bf16[16,128,512]{2,1,0:T(8,128)(2,1)}), bf16[16,128,512]{2,1,0:T(8,128)(2,1)}, u32[]{:S(2)}, u32[]{:S(2)}) async-start(bf16[16,128,512]{2,1,0:T(8,128)(2,1)} %bitcast.409), calls=%async_computation.4 | async-start | bytes 4194304 | tf_op jit(solution)/shard_map/all_to_all | solution.py:220
  402.6 289.6 %copy-start.135 = (f32[512]{0:T(512)}, f32[512]{0:T(512)S(1)}, u32[]{:S(2)}) copy-start(f32[512]{0:T(512)S(1)} %get-tuple-element.276) | copy-start | bytes 6148
  418.8 36.7 %copy-start.113 = (f32[512]{0:T(512)S(1)}, f32[512]{0:T(512)}, u32[]{:S(2)}) copy-start(f32[512]{0:T(512)} %param.26) | copy-start | bytes 6148
  418.8 36.7 %copy-start.116 = (f32[512]{0:T(512)S(1)}, f32[512]{0:T(512)}, u32[]{:S(2)}) copy-start(f32[512]{0:T(512)} %copy-done.115) | copy-start | bytes 6148
  418.8 36.7 %copy-start.133 = (f32[512]{0:T(512)S(1)}, f32[512]{0:T(512)}, u32[]{:S(2)}) copy-start(f32[512]{0:T(512)} %copy-done.132) | copy-start | bytes 6148
  418.8 36.7 %copy-start.177 = (f32[512]{0:T(512)S(1)}, f32[512]{0:T(512)}, u32[]{:S(2)}) copy-start(f32[512]{0:T(512)} %param.27) | copy-start | bytes 6148
  418.8 37.7 %copy-start.27 = (f32[512,512]{1,0:T(8,128)S(1)}, f32[512,512]{1,0:T(8,128)}, u32[]{:S(2)}) copy-start(f32[512,512]{1,0:T(8,128)} %copy-done.26) | copy-start | bytes 3145732
  449.6 52.2 %all-to-all-start.6 = ((bf16[16,128,512]{2,1,0:T(8,128)(2,1)}), bf16[16,128,512]{2,1,0:T(8,128)(2,1)}, u32[]{:S(2)}, u32[]{:S(2)}) async-start(bf16[16,128,512]{2,1,0:T(8,128)(2,1)} %bitcast.408), calls=%async_computation.6 | async-start | bytes 4194304 | tf_op jit(solution)/shard_map/all_to_all | solution.py:220
  454.0 371.6 %reduce-scatter.5.cloned.1.call-start = ((), (), s32[]{:S(2)}) async-start(), calls=%async_computation.13 | async-start | bytes 5242880 | tf_op jit(solution)/shard_map/reduce_scatter | solution.py:317
  518.0 20.5 %copy-start.203 = (bf16[2,512,2048]{2,1,0:T(8,128)(2,1)S(1)}, bf16[2,512,2048]{2,1,0:T(8,128)(2,1)}, u32[]{:S(2)}) copy-start(bf16[2,512,2048]{2,1,0:T(8,128)(2,1)} %all-gather.3.cloned.1.call-done) | copy-start | bytes 12582916
  550.5 52.4 %all-to-all-start.7 = ((bf16[2,1024,512]{2,0,1:T(2,128)(2,1)}), bf16[2,1024,512]{2,0,1:T(2,128)(2,1)}, u32[]{:S(2)}, u32[]{:S(2)}) async-start(bf16[2,1024,512]{2,0,1:T(2,128)(2,1)} %copy.656), calls=%async_computation.7 | async-start | bytes 4194304 | tf_op jit(solution)/shard_map/all_to_all | solution.py:233
  555.3 19.9 %copy-start.204 = (bf16[2,512,2048]{2,1,0:T(8,128)(2,1)S(1)}, bf16[2,512,2048]{2,1,0:T(8,128)(2,1)}, u32[]{:S(2)}) copy-start(bf16[2,512,2048]{2,1,0:T(8,128)(2,1)} %all-gather.3.cloned.1.call-done) | copy-start | bytes 12582916
  587.2 21.3 %copy-start.41 = (bf16[512,512]{0,1:T(8,128)(2,1)S(1)}, bf16[512,512]{0,1:T(8,128)(2,1)}, u32[]{:S(2)}) copy-start(bf16[512,512]{0,1:T(8,128)(2,1)} %get-tuple-element.328) | copy-start | bytes 1572868
  587.2 21.5 %copy-start.39 = (bf16[512,512]{0,1:T(8,128)(2,1)S(1)}, bf16[512,512]{0,1:T(8,128)(2,1)}, u32[]{:S(2)}) copy-start(bf16[512,512]{0,1:T(8,128)(2,1)} %copy-done.38) | copy-start | bytes 1572868
  602.9 52.2 %all-to-all-start.5 = ((bf16[2,1024,512]{2,0,1:T(2,128)(2,1)}), bf16[2,1024,512]{2,0,1:T(2,128)(2,1)}, u32[]{:S(2)}, u32[]{:S(2)}) async-start(bf16[2,1024,512]{2,0,1:T(2,128)(2,1)} %copy.634), calls=%async_computation.5 | async-start | bytes 4194304 | tf_op jit(solution)/shard_map/all_to_all | solution.py:233
  607.3 221.2 %reduce-scatter.3.cloned.1.call-start = ((), (), s32[]{:S(2)}) async-start(), calls=%async_computation.12 | async-start | bytes 5242880 | tf_op jit(solution)/shard_map/reduce_scatter | solution.py:314
  627.3 296.2 %all-reduce.5.cloned.1.call-start = ((), (), s32[]{:S(2)}) async-start(), calls=%async_computation.14 | async-start | bytes 13107200 | tf_op jit(solution)/shard_map/psum | solution.py:295
  636.6 21.8 %copy-start.141 = (s32[1024]{0:T(1024)S(1)}, s32[1024]{0:T(1024)}, u32[]{:S(2)}) copy-start(s32[1024]{0:T(1024)} %copy-done.140) | copy-start | bytes 12292
  678.8 9.3 copy-start.10
  678.8 9.3 copy-start.127
  678.8 9.3 copy-start.129
  678.8 9.3 copy-start.150
  (174 other events, 692.8 us)
Sparse Core Ops, SparseCore 0:
  9.6 37.1 all-gather.2
  48.4 34.5 all-gather.4
  518.1 43.5 reduce-scatter.4
  627.4 45.7 reduce-scatter.2
  764.6 158.8 all-reduce.4
where the time goes:
time: 944 us; the launch traced here: 937 us
  waiting for transfers between devices  270 us (29%)
  local copies, waits for them, and re-layouts  224 us (24%)
  matrix products  212 us (22%)
  other arithmetic  133 us (14%)
  blocking collectives  40.2 us (4%)
  starting transfers between devices  39.6 us (4%)
  between operations  18.8 us (2%)
    psum x1, waiting for transfers between devices, per_device(): lax.psum((grad_gain_one, grad_bias_one, grad_router_attn, grad_query_w, g...  92.1 us
    all_to_all x2, waiting for transfers between devices, per_device(): lax.all_to_all(grad_buffer.reshape(experts_all, capacity, width), 'expert...  53.6 us
    all_to_all x2, waiting for transfers between devices, per_device(): lax.all_to_all(outgoing.reshape(experts_all, capacity, width), 'expert',...  47.6 us
    all_to_all x2, waiting for transfers between devices, per_device(): lax.all_to_all(outgoing_back, 'expert', split_axis=1, concat_axis=0, tile...  41.4 us
    dot_general x2, matrix products, expert_backward(): jnp.einsum('erd,efd->erf', grad_rows_in, second, preferred_element_type=j...  40.4 us
    psum x1, blocking collectives, per_device(): lax.psum((grad_gain_one, grad_bias_one, grad_router_attn, grad_query_w, g...  40.2 us
    all_to_all x2, waiting for transfers between devices, per_device(): lax.all_to_all(back_rows, 'expert', split_axis=1, concat_axis=0, tiled=True)  34.2 us
    unnamed x431, local copies, waits for them, and re-layouts  27 us
  transfers between devices with their start and end apart: 13, of which 9 were waited for; matrix products, arithmetic and copies ran while one was open for 53% of the time, Pallas kernels for 0%

commit v1 on v0

--- a/solution.py
+++ b/solution.py
@@ -292,23 +292,22 @@
         grads_in.append(grad_state + grad_in_norm)
         grad_halt_w = jnp.sum(grad_halt * state_end, axis=0)
         grad_halt_b = jnp.sum(grad_halt, axis=0)
-        summed = lax.psum(
-            (
-                grad_gain_one,
-                grad_bias_one,
-                grad_router_attn,
-                grad_query_w,
-                grad_key_w,
-                grad_value_w,
-                grad_proj,
-                grad_gain_two,
-                grad_bias_two,
-                grad_router_ffn,
-                grad_halt_w,
-                grad_halt_b,
-            ),
-            ("expert", "hidden"),
-        )
+        summed = (
+            grad_gain_one,
+            grad_bias_one,
+            grad_router_attn,
+            grad_query_w,
+            grad_key_w,
+            grad_value_w,
+            grad_proj,
+            grad_gain_two,
+            grad_bias_two,
+            grad_router_ffn,
+            grad_halt_w,
+            grad_halt_b,
+        )
+        for mesh_axis in ("hidden", "expert"):
+            summed = lax.psum(summed, mesh_axis)
         totals = tuple(jax.tree.map(jnp.add, totals, tuple(summed)))
     acc_in, acc_out = (
         lax.psum_scatter(

time: 944 us -> 1210 us (1.28)
  waiting for transfers between devices: 270 us -> 515 us
  blocking collectives: 40.2 us -> 53.5 us
    psum x1 -> x2, waiting for transfers between devices: 92.1 us -> 296 us  [per_device(): summed = lax.psum(summed, mesh_axis)]
    all_to_all x2, waiting for transfers between devices: 53.6 us -> 75.5 us  [per_device(): lax.all_to_all(grad_buffer.reshape(experts_all, capacity, width), 'expert...]
    psum x1 -> x2, blocking collectives: 40.2 us -> 53.5 us  [per_device(): summed = lax.psum(summed, mesh_axis)]
    all_to_all x2, waiting for transfers between devices: 34.2 us -> 46.7 us  [per_device(): lax.all_to_all(back_rows, 'expert', split_axis=1, concat_axis=0, tiled=True)]
    unnamed x431 -> x425, local copies, waits for them, and re-layouts: 27 us -> 26.9 us
  transfers between devices with their start and end apart: 13 -> 14, of which waited for: 9 -> 11; matrix products, arithmetic and copies ran while one was open for 53% -> 32% of each run, Pallas kernels for 0% -> 0%
where the time goes in v1:
time: 1210 us; the launch traced here: 1200 us
  waiting for transfers between devices  515 us (43%)
  local copies, waits for them, and re-layouts  226 us (19%)
  matrix products  216 us (18%)
  other arithmetic  132 us (11%)
  blocking collectives  53.5 us (4%)
  starting transfers between devices  40 us (3%)
  between operations  19.1 us (2%)
    psum x2, waiting for transfers between devices, per_device(): summed = lax.psum(summed, mesh_axis)  296 us
    all_to_all x2, waiting for transfers between devices, per_device(): lax.all_to_all(grad_buffer.reshape(experts_all, capacity, width), 'expert...  75.5 us
    psum x2, blocking collectives, per_device(): summed = lax.psum(summed, mesh_axis)  53.5 us
    all_to_all x2, waiting for transfers between devices, per_device(): lax.all_to_all(outgoing.reshape(experts_all, capacity, width), 'expert',...  47.6 us
    all_to_all x2, waiting for transfers between devices, per_device(): lax.all_to_all(back_rows, 'expert', split_axis=1, concat_axis=0, tiled=True)  46.7 us
    all_to_all x2, waiting for transfers between devices, per_device(): lax.all_to_all(outgoing_back, 'expert', split_axis=1, concat_axis=0, tile...  41.4 us
    dot_general x2, matrix products, expert_backward(): jnp.einsum('erd,efd->erf', grad_rows_in, second, preferred_element_type=j...  36.8 us
    unnamed x425, local copies, waits for them, and re-layouts  26.9 us
  transfers between devices with their start and end apart: 14, of which 11 were waited for; matrix products, arithmetic and copies ran while one was open for 32% of the time, Pallas kernels for 0%

profile of v1, /device:TPU:0, one launch (start us, length us, event | category | flops | bytes accessed | tf_op | source)
XLA Modules:
  0.0 1201.1 jit_solution(11296982589351600339)
XLA Ops:
  26.7 8.9 select_reduce_fusion.3
  38.3 8.9 select_reduce_fusion.2
  89.7 4.9 copy.590
  102.4 5.1 copy.613
  133.6 7.2 scatter_custom_fusion.1
  140.8 7.4 all-to-all-start.2
  159.8 7.2 scatter_custom_fusion
  167.0 29.6 %all-to-all-done.2 = bf16[16,128,512]{2,1,0:T(8,128)(2,1)} async-done(((bf16[16,128,512]{2,1,0:T(8,128)(2,1)}), bf16[16,128,512]{2,1,0:T(8,128)(2,1)}, u32[]{:S(2)}, u32[]{:S(2)}) %all-to-all-start.2) | async-done | bytes 2097184 | tf_op jit(solution)/shard_map/all_to_all | solution.py:196
  196.6 4.5 all-to-all-start
  204.2 13.1 %fusion.188 = f32[2,1024,2048]{2,1,0:T(8,128)} fusion(bf16[2,1024,512]{2,1,0:T(8,128)(2,1)} %bitcast.422, bf16[2,512,2048]{2,1,0:T(8,128)(2,1)} %all-gather.3.cloned.1.call-done), kind=kOutput, calls=%fused_computation.370 | convolution fusion | flops 4294967296 | bytes 23068672 | tf_op jit(solution)/shard_map/erd,edf->erf/dot_general | solution.py:80
  217.3 10.1 convolution_convert_fusion.6
  230.9 18.0 %all-to-all-done = bf16[16,128,512]{2,1,0:T(8,128)(2,1)} async-done(((bf16[16,128,512]{2,1,0:T(8,128)(2,1)}), bf16[16,128,512]{2,1,0:T(8,128)(2,1)}, u32[]{:S(2)}, u32[]{:S(2)}) %all-to-all-start) | async-done | bytes 2097184 | tf_op jit(solution)/shard_map/all_to_all | solution.py:196
  248.9 4.6 all-to-all-start.3
  256.3 10.4 multiply_convert_fusion.1
  266.7 4.7 convolution_convert_fusion.7
  274.9 26.4 %all-to-all-done.3 = bf16[2,1024,512]{2,0,1:T(2,128)(2,1)} async-done(((bf16[2,1024,512]{2,0,1:T(2,128)(2,1)}), bf16[2,1024,512]{2,0,1:T(2,128)(2,1)}, u32[]{:S(2)}, u32[]{:S(2)}) %all-to-all-start.3) | async-done | bytes 2097184 | tf_op jit(solution)/shard_map/all_to_all | solution.py:205
  301.3 4.6 all-to-all-start.1
  320.5 7.0 gather_fusion.1
  330.8 5.4 multiply_reduce_fusion.4
  338.7 15.0 %all-to-all-done.1 = bf16[2,1024,512]{2,0,1:T(2,128)(2,1)} async-done(((bf16[2,1024,512]{2,0,1:T(2,128)(2,1)}), bf16[2,1024,512]{2,0,1:T(2,128)(2,1)}, u32[]{:S(2)}, u32[]{:S(2)}) %all-to-all-start.1) | async-done | bytes 2097184 | tf_op jit(solution)/shard_map/all_to_all | solution.py:205
  357.0 7.0 gather_fusion
  367.3 5.4 multiply_reduce_fusion.5
  388.0 8.2 scatter_custom_fusion.2
  409.9 7.7 scatter_custom_fusion.3
  417.7 30.9 %all-to-all-done.4 = bf16[16,128,512]{2,1,0:T(8,128)(2,1)} async-done(((bf16[16,128,512]{2,1,0:T(8,128)(2,1)}), bf16[16,128,512]{2,1,0:T(8,128)(2,1)}, u32[]{:S(2)}, u32[]{:S(2)}) %all-to-all-start.4) | async-done | bytes 2097184 | tf_op jit(solution)/shard_map/all_to_all | solution.py:220
  456.2 44.6 %all-to-all-done.6 = bf16[16,128,512]{2,1,0:T(8,128)(2,1)} async-done(((bf16[16,128,512]{2,1,0:T(8,128)(2,1)}), bf16[16,128,512]{2,1,0:T(8,128)(2,1)}, u32[]{:S(2)}, u32[]{:S(2)}) %all-to-all-start.6) | async-done | bytes 2097184 | tf_op jit(solution)/shard_map/all_to_all | solution.py:220
  503.7 17.0 %fusion.13 = bf16[2,1024,2048]{2,1,0:T(8,128)(2,1)} fusion(f32[2,1024,2048]{2,1,0:T(8,128)} %fusion.188, bf16[2,1024,512]{2,1,0:T(8,128)(2,1)S(1)} %bitcast.428, bf16[2,2048,512]{2,1,0:T(8,128)(2,1)S(1)} %copy-done.202), kind=kOutput, calls=%fused_computation.25 | convolution fusion | flops 4378853376 | bytes 31457280 | tf_op jit(solution)/shard_map/erd,efd->erf/dot_general | solution.py:87
  520.7 9.1 convolution_convert_fusion.4
  533.3 4.6 all-to-all-start.7
  537.9 19.8 %fusion.6 = bf16[2,1024,2048]{2,1,0:T(8,128)(2,1)} fusion(f32[2,1024,2048]{2,1,0:T(8,128)} %get-tuple-element.371, bf16[2,1024,512]{2,1,0:T(8,128)(2,1)} %bitcast.426, bf16[2,2048,512]{2,1,0:T(8,128)(2,1)} %all-gather.5.cloned.1.call-done), kind=kOutput, calls=%fused_computation.18 | convolution fusion | flops 4378853376 | bytes 31457280 | tf_op jit(solution)/shard_map/erd,efd->erf/dot_general | solution.py:87
  557.7 8.5 convolution_convert_fusion.5
  569.7 15.9 %all-to-all-done.7 = bf16[2,1024,512]{2,0,1:T(2,128)(2,1)} async-done(((bf16[2,1024,512]{2,0,1:T(2,128)(2,1)}), bf16[2,1024,512]{2,0,1:T(2,128)(2,1)}, u32[]{:S(2)}, u32[]{:S(2)}) %all-to-all-start.7) | async-done | bytes 2097184 | tf_op jit(solution)/shard_map/all_to_all | solution.py:233
  601.2 5.8 gather_fusion.3
  607.0 30.8 %all-to-all-done.5 = bf16[2,1024,512]{2,0,1:T(2,128)(2,1)} async-done(((bf16[2,1024,512]{2,0,1:T(2,128)(2,1)}), bf16[2,1024,512]{2,0,1:T(2,128)(2,1)}, u32[]{:S(2)}, u32[]{:S(2)}) %all-to-all-start.5) | async-done | bytes 2097184 | tf_op jit(solution)/shard_map/all_to_all | solution.py:233
  641.1 7.0 gather_fusion.2
  651.5 5.1 reduce_sum.693
  661.6 5.1 reduce_sum.706
  686.9 4.9 copy.663
  708.9 5.3 copy.641
  741.4 11.9 fusion.194
  753.4 13.3 %add_convert_fusion = bf16[2,2048,512]{2,1,0:T(8,128)(2,1)} fusion(f32[2,2048,512]{2,1,0:T(8,128)} %fusion.194, bf16[2,1024,512]{2,1,0:T(8,128)(2,1)S(1)} %bitcast.429, f32[2,1024,2048]{2,1,0:T(8,128)} %fusion.188), kind=kOutput, calls=%fused_computation.28 | convolution fusion | flops 4336910336 | bytes 31457280 | tf_op jit(solution)/shard_map/erf,erd->efd/dot_general | solution.py:89
  766.8 7.9 fusion.193
  774.7 9.9 add_convert_fusion.1
  793.1 71.7 %all-reduce.11.cloned.1.call-done = (f32[512,1536]{1,0:T(8,128)}, f32[512,64]{0,1:T(8,128)}, f32[512,64]{0,1:T(8,128)}, f32[1536,512]{1,0:T(8,128)}) async-done(((f32[512,1536]{1,0:T(8,128)}, f32[512,64]{0,1:T(8,128)}, f32[512,64]{0,1:T(8,128)}, f32[1536,512]{1,0:T(8,128)}), (f32[512,1536]{1,0:T(8,128)}, f32[512,64]{0,1:T(8,128)}, f32[512,64]{0,1:T(8,128)}, ...) | async-done | bytes 6553616 | tf_op jit(solution)/shard_map/psum | solution.py:310
  897.6 15.0 %all-reduce.12 = (f32[512]{0:T(512)S(1)}, f32[512]{0:T(512)S(1)}, f32[512,24]{0,1:T(8,128)S(1)}, f32[512]{0:T(512)S(1)}, f32[512]{0:T(512)S(1)}, /*index=5*/f32[512,16]{0,1:T(8,128)S(1)}, f32[512]{0:T(512)S(1)}, f32[1]{0:T(128)}) all-reduce(f32[512]{0:T(512)S(1)} %add.652, ...), channel_id=1, replica_groups=mesh['expert'=8,'hidden'=4] {'hidden'}, use_global_device_ids=true, to_apply=%region_65.66 | all-reduce | flops 23041 | bytes 184328 | tf_op jit(solution)/shard_map/psum | solution.py:310
  912.5 38.5 %all-reduce.13 = (f32[512]{0:T(512)}, f32[512]{0:T(512)}, f32[512,24]{0,1:T(8,128)}, f32[512]{0:T(512)}, f32[512]{0:T(512)}, /*index=5*/f32[512,16]{0,1:T(8,128)}, f32[512]{0:T(512)}, f32[1]{0:T(128)}) all-reduce(f32[512]{0:T(512)S(1)} %get-tuple-element.274, ...), channel_id=1, replica_groups=mesh['expert'=8,'hidden'=4] {'expert'}, use_global_device_ids=true, to_apply=%region_66.67 | all-reduce | flops 23041 | bytes 184328 | tf_op jit(solution)/shard_map/psum | solution.py:310
  953.9 6.6 reduce-scatter.3.cloned.1.call-done
  963.3 223.8 %all-reduce.9.cloned.1.call-done = (f32[512,1536]{1,0:T(8,128)}, f32[512,64]{0,1:T(8,128)}, f32[512,64]{0,1:T(8,128)}, f32[1536,512]{1,0:T(8,128)}) async-done(((f32[512,1536]{1,0:T(8,128)}, f32[512,64]{0,1:T(8,128)}, f32[512,64]{0,1:T(8,128)}, f32[1536,512]{1,0:T(8,128)}), (f32[512,1536]{1,0:T(8,128)}, f32[512,64]{0,1:T(8,128)}, f32[512,64]{0,1:T(8,128)}, ...) | async-done | bytes 6553616 | tf_op jit(solution)/shard_map/psum | solution.py:310
  (688 shorter events, 337.9 us)
Async XLA Ops:
  7.2 110.9 %copy-start = (bf16[1536,512]{1,0:T(8,128)(2,1)S(1)}, bf16[1536,512]{1,0:T(8,128)(2,1)}, u32[]{:S(2)}) copy-start(bf16[1536,512]{1,0:T(8,128)(2,1)} %param.32) | copy-start | bytes 4718596
  7.2 197.0 %all-gather.3.cloned.1.call-start = ((), (), s32[]{:S(2)}) async-start(), calls=%async_computation.10 | async-start | bytes 5242880 | tf_op jit(solution)/shard_map/all_gather | solution.py:127
  7.9 209.4 %all-gather.5.cloned.1.call-start = ((), (), s32[]{:S(2)}) async-start(), calls=%async_computation.11 | async-start | bytes 5242880 | tf_op jit(solution)/shard_map/all_gather | solution.py:128
  14.3 364.6 %copy-start.5 = (bf16[1,512,512]{1,2,0:T(8,128)(2,1)}, bf16[1,512,512]{1,2,0:T(8,128)(2,1)S(1)}, u32[]{:S(2)}) copy-start(bf16[1,512,512]{1,2,0:T(8,128)(2,1)S(1)} %copy.705) | copy-start | bytes 1572868
  15.6 38.3 %copy-start.13 = (bf16[512,512]{0,1:T(8,128)(2,1)}, bf16[512,512]{0,1:T(8,128)(2,1)S(1)}, u32[]{:S(2)}) copy-start(bf16[512,512]{0,1:T(8,128)(2,1)S(1)} %get-tuple-element.345) | copy-start | bytes 1572868
  15.8 103.6 %copy-start.68 = (bf16[512,64,1]{0,1,2:T(8,128)(2,1)}, bf16[512,64,1]{0,1,2:T(8,128)(2,1)S(1)}, u32[]{:S(2)}) copy-start(bf16[512,64,1]{0,1,2:T(8,128)(2,1)S(1)} %fusion.62) | copy-start | bytes 196612
  16.9 96.7 %copy-start.70 = (bf16[512,64,1]{0,1,2:T(8,128)(2,1)}, bf16[512,64,1]{0,1,2:T(8,128)(2,1)S(1)}, u32[]{:S(2)}) copy-start(bf16[512,64,1]{0,1,2:T(8,128)(2,1)S(1)} %fusion.64) | copy-start | bytes 196612
  20.0 74.6 %copy-start.42 = (s32[512,4]{1,0:T(8,128)}, s32[512,4]{1,0:T(8,128)S(1)}, u32[]{:S(2)}) copy-start(s32[512,4]{1,0:T(8,128)S(1)} %copy.585) | copy-start | bytes 24580
  36.6 47.2 %copy-start.103 = (f32[512,4]{0,1:T(4,128)}, f32[512,4]{0,1:T(4,128)S(1)}, u32[]{:S(2)}) copy-start(f32[512,4]{0,1:T(4,128)S(1)} %copy.588) | copy-start | bytes 24580
  50.0 36.4 %copy-start.101 = (f32[512,4]{0,1:T(4,128)}, f32[512,4]{0,1:T(4,128)S(1)}, u32[]{:S(2)}) copy-start(f32[512,4]{0,1:T(4,128)S(1)} %copy.611) | copy-start | bytes 24580
  87.1 28.0 %copy-start.125 = (f32[512,4]{0,1:T(4,128)}, f32[512,4]{0,1:T(4,128)S(1)}, u32[]{:S(2)}) copy-start(f32[512,4]{0,1:T(4,128)S(1)} %fusion.156) | copy-start | bytes 24580
  99.7 19.7 %copy-start.51 = (bf16[512,4,64]{0,2,1:T(8,128)(2,1)}, bf16[512,4,64]{0,2,1:T(8,128)(2,1)S(1)}, u32[]{:S(2)}) copy-start(bf16[512,4,64]{0,2,1:T(8,128)(2,1)S(1)} %copy.591) | copy-start | bytes 786436
  127.2 13.6 %copy-start.35 = (bf16[512,512]{0,1:T(8,128)(2,1)}, bf16[512,512]{0,1:T(8,128)(2,1)S(1)}, u32[]{:S(2)}) copy-start(bf16[512,512]{0,1:T(8,128)(2,1)S(1)} %get-tuple-element.341) | copy-start | bytes 1572868
  133.6 14.6 %copy-start.186 = (s32[1,512,2]{1,2,0:T(2,128)S(1)}, s32[1,512,2]{1,2,0:T(2,128)}, u32[]{:S(2)}) copy-start(s32[1,512,2]{1,2,0:T(2,128)} %get-tuple-element.339) | copy-start | bytes 12292
  133.6 15.1 %copy-start.185 = (s32[1,512,2]{1,2,0:T(2,128)S(1)}, s32[1,512,2]{1,2,0:T(2,128)}, u32[]{:S(2)}) copy-start(s32[1,512,2]{1,2,0:T(2,128)} %get-tuple-element.335) | copy-start | bytes 12292
  140.8 13.1 %copy-start.36 = (bf16[512,512]{0,1:T(8,128)(2,1)S(1)}, bf16[512,512]{0,1:T(8,128)(2,1)}, u32[]{:S(2)}) copy-start(bf16[512,512]{0,1:T(8,128)(2,1)} %get-tuple-element.340) | copy-start | bytes 1572868
  140.8 55.8 %all-to-all-start.2 = ((bf16[16,128,512]{2,1,0:T(8,128)(2,1)}), bf16[16,128,512]{2,1,0:T(8,128)(2,1)}, u32[]{:S(2)}, u32[]{:S(2)}) async-start(bf16[16,128,512]{2,1,0:T(8,128)(2,1)} %bitcast.410), calls=%async_computation.2 | async-start | bytes 4194304 | tf_op jit(solution)/shard_map/all_to_all | solution.py:196
  196.6 52.3 %all-to-all-start = ((bf16[16,128,512]{2,1,0:T(8,128)(2,1)}), bf16[16,128,512]{2,1,0:T(8,128)(2,1)}, u32[]{:S(2)}, u32[]{:S(2)}) async-start(bf16[16,128,512]{2,1,0:T(8,128)(2,1)} %bitcast.411), calls=%async_computation | async-start | bytes 4194304 | tf_op jit(solution)/shard_map/all_to_all | solution.py:196
  248.9 52.4 %all-to-all-start.3 = ((bf16[2,1024,512]{2,0,1:T(2,128)(2,1)}), bf16[2,1024,512]{2,0,1:T(2,128)(2,1)}, u32[]{:S(2)}, u32[]{:S(2)}) async-start(bf16[2,1024,512]{2,0,1:T(2,128)(2,1)} %copy.627), calls=%async_computation.3 | async-start | bytes 4194304 | tf_op jit(solution)/shard_map/all_to_all | solution.py:205
  301.3 52.4 %all-to-all-start.1 = ((bf16[2,1024,512]{2,0,1:T(2,128)(2,1)}), bf16[2,1024,512]{2,0,1:T(2,128)(2,1)}, u32[]{:S(2)}, u32[]{:S(2)}) async-start(bf16[2,1024,512]{2,0,1:T(2,128)(2,1)} %copy.604), calls=%async_computation.1 | async-start | bytes 4194304 | tf_op jit(solution)/shard_map/all_to_all | solution.py:205
  310.1 68.9 %copy-start.17 = (bf16[1,512,512]{1,2,0:T(8,128)(2,1)}, bf16[1,512,512]{1,2,0:T(8,128)(2,1)S(1)}, u32[]{:S(2)}) copy-start(bf16[1,512,512]{1,2,0:T(8,128)(2,1)S(1)} %copy.706) | copy-start | bytes 1572868
  378.9 295.9 %copy-start.134 = (f32[512]{0:T(512)}, f32[512]{0:T(512)S(1)}, u32[]{:S(2)}) copy-start(f32[512]{0:T(512)S(1)} %get-tuple-element.291) | copy-start | bytes 6148
  378.9 295.9 %copy-start.148 = (f32[512]{0:T(512)}, f32[512]{0:T(512)S(1)}, u32[]{:S(2)}) copy-start(f32[512]{0:T(512)S(1)} %get-tuple-element.290) | copy-start | bytes 6148
  396.2 52.3 %all-to-all-start.4 = ((bf16[16,128,512]{2,1,0:T(8,128)(2,1)}), bf16[16,128,512]{2,1,0:T(8,128)(2,1)}, u32[]{:S(2)}, u32[]{:S(2)}) async-start(bf16[16,128,512]{2,1,0:T(8,128)(2,1)} %bitcast.408), calls=%async_computation.4 | async-start | bytes 4194304 | tf_op jit(solution)/shard_map/all_to_all | solution.py:220
  401.5 273.4 %copy-start.140 = (f32[512]{0:T(512)}, f32[512]{0:T(512)S(1)}, u32[]{:S(2)}) copy-start(f32[512]{0:T(512)S(1)} %get-tuple-element.288) | copy-start | bytes 6148
  401.5 273.4 %copy-start.161 = (f32[512]{0:T(512)}, f32[512]{0:T(512)S(1)}, u32[]{:S(2)}) copy-start(f32[512]{0:T(512)S(1)} %get-tuple-element.287) | copy-start | bytes 6148
  448.5 52.3 %all-to-all-start.6 = ((bf16[16,128,512]{2,1,0:T(8,128)(2,1)}), bf16[16,128,512]{2,1,0:T(8,128)(2,1)}, u32[]{:S(2)}, u32[]{:S(2)}) async-start(bf16[16,128,512]{2,1,0:T(8,128)(2,1)} %bitcast.409), calls=%async_computation.6 | async-start | bytes 4194304 | tf_op jit(solution)/shard_map/all_to_all | solution.py:220
  502.7 18.0 %copy-start.59 = (bf16[2,8,128,512]{3,2,1,0:T(8,128)(2,1)}, bf16[2,8,128,512]{3,2,1,0:T(8,128)(2,1)S(1)}, u32[]{:S(2)}) copy-start(bf16[2,8,128,512]{3,2,1,0:T(8,128)(2,1)S(1)} %copy.655) | copy-start | bytes 6291460
  533.3 52.4 %all-to-all-start.7 = ((bf16[2,1024,512]{2,0,1:T(2,128)(2,1)}), bf16[2,1024,512]{2,0,1:T(2,128)(2,1)}, u32[]{:S(2)}, u32[]{:S(2)}) async-start(bf16[2,1024,512]{2,0,1:T(2,128)(2,1)} %copy.656), calls=%async_computation.7 | async-start | bytes 4194304 | tf_op jit(solution)/shard_map/all_to_all | solution.py:233
  537.8 19.8 %copy-start.200 = (bf16[2,512,2048]{2,1,0:T(8,128)(2,1)S(1)}, bf16[2,512,2048]{2,1,0:T(8,128)(2,1)}, u32[]{:S(2)}) copy-start(bf16[2,512,2048]{2,1,0:T(8,128)(2,1)} %all-gather.3.cloned.1.call-done) | copy-start | bytes 12582916
  569.7 20.8 %copy-start.120 = (f32[512,4]{0,1:T(4,128)S(1)}, f32[512,4]{0,1:T(4,128)}, u32[]{:S(2)}) copy-start(f32[512,4]{0,1:T(4,128)} %copy-done.119) | copy-start | bytes 24580
  569.7 20.8 %copy-start.155 = (f32[512,4]{0,1:T(4,128)S(1)}, f32[512,4]{0,1:T(4,128)}, u32[]{:S(2)}) copy-start(f32[512,4]{0,1:T(4,128)} %copy-done.154) | copy-start | bytes 24580
  569.7 20.8 %copy-start.122 = (f32[512,4]{0,1:T(4,128)S(1)}, f32[512,4]{0,1:T(4,128)}, u32[]{:S(2)}) copy-start(f32[512,4]{0,1:T(4,128)} %copy-done.121) | copy-start | bytes 24580
  569.7 20.8 %copy-start.157 = (f32[512,4]{0,1:T(4,128)S(1)}, f32[512,4]{0,1:T(4,128)}, u32[]{:S(2)}) copy-start(f32[512,4]{0,1:T(4,128)} %copy-done.156) | copy-start | bytes 24580
  569.7 20.8 %copy-start.111 = (f32[512]{0:T(512)S(1)}, f32[512]{0:T(512)}, u32[]{:S(2)}) copy-start(f32[512]{0:T(512)} %param.26) | copy-start | bytes 6148
  569.7 20.8 %copy-start.114 = (f32[512]{0:T(512)S(1)}, f32[512]{0:T(512)}, u32[]{:S(2)}) copy-start(f32[512]{0:T(512)} %copy-done.113) | copy-start | bytes 6148
  569.7 20.8 %copy-start.138 = (f32[512]{0:T(512)S(1)}, f32[512]{0:T(512)}, u32[]{:S(2)}) copy-start(f32[512]{0:T(512)} %copy-done.137) | copy-start | bytes 6148
  569.7 20.8 %copy-start.179 = (f32[512]{0:T(512)S(1)}, f32[512]{0:T(512)}, u32[]{:S(2)}) copy-start(f32[512]{0:T(512)} %param.27) | copy-start | bytes 6148
  569.7 21.9 %copy-start.27 = (f32[512,512]{1,0:T(8,128)S(1)}, f32[512,512]{1,0:T(8,128)}, u32[]{:S(2)}) copy-start(f32[512,512]{1,0:T(8,128)} %copy-done.26) | copy-start | bytes 3145732
  585.7 52.2 %all-to-all-start.5 = ((bf16[2,1024,512]{2,0,1:T(2,128)(2,1)}), bf16[2,1024,512]{2,0,1:T(2,128)(2,1)}, u32[]{:S(2)}, u32[]{:S(2)}) async-start(bf16[2,1024,512]{2,0,1:T(2,128)(2,1)} %copy.634), calls=%async_computation.5 | async-start | bytes 4194304 | tf_op jit(solution)/shard_map/all_to_all | solution.py:233
  590.0 274.8 %all-reduce.11.cloned.1.call-start = ((), (), s32[]{:S(2)}) async-start(), calls=%async_computation.15 | async-start | bytes 13107200 | tf_op jit(solution)/shard_map/psum | solution.py:310
  597.7 73.0 %copy-start.105 = (bf16[512,16]{0,1:T(8,128)(2,1)}, bf16[512,16]{0,1:T(8,128)(2,1)S(1)}, u32[]{:S(2)}) copy-start(bf16[512,16]{0,1:T(8,128)(2,1)S(1)} %select_reduce_fusion.5) | copy-start | bytes 49156
  597.8 71.4 %copy-start.106 = (bf16[512,16]{0,1:T(8,128)(2,1)}, bf16[512,16]{0,1:T(8,128)(2,1)S(1)}, u32[]{:S(2)}) copy-start(bf16[512,16]{0,1:T(8,128)(2,1)S(1)} %select_reduce_fusion.4) | copy-start | bytes 49156
  741.2 209.8 %reduce-scatter.5.cloned.1.call-start = ((), (), s32[]{:S(2)}) async-start(), calls=%async_computation.13 | async-start | bytes 5242880 | tf_op jit(solution)/shard_map/reduce_scatter | solution.py:316
  741.4 12.0 copy-start.60
  766.8 193.7 %reduce-scatter.3.cloned.1.call-start = ((), (), s32[]{:S(2)}) async-start(), calls=%async_computation.12 | async-start | bytes 5242880 | tf_op jit(solution)/shard_map/reduce_scatter | solution.py:313
  784.6 402.5 %all-reduce.9.cloned.1.call-start = ((), (), s32[]{:S(2)}) async-start(), calls=%async_computation.14 | async-start | bytes 13107200 | tf_op jit(solution)/shard_map/psum | solution.py:310
  791.8 73.0 %copy-start.127 = (f32[512,4]{0,1:T(4,128)}, f32[512,4]{0,1:T(4,128)S(1)}, u32[]{:S(2)}) copy-start(f32[512,4]{0,1:T(4,128)S(1)} %multiply_reduce_fusion.17) | copy-start | bytes 24580
  (172 other events, 636.1 us)
Sparse Core Ops, SparseCore 0:
  9.6 37.2 all-gather.2
  48.4 34.4 all-gather.4
  741.3 123.3 all-reduce.10
  867.1 46.1 reduce-scatter.4
  915.9 44.5 reduce-scatter.2
  964.9 222.2 all-reduce.8
